TPU v7x, 256 devices: a whole 4x4x8 slice. The times are simulated.
256 devices in a mesh: proc: 32 (over x, z), rep: 8 (over y, core).
Axes of the slice: x: 4, y: 4, z: 8, core: 2. Of those that a mesh axis runs over, the one named last changes fastest.
Arguments:
- amplitudes: bfloat16 [512, 208, 128], P('proc'), may hold values from -6 to 6
- ladder_rows: int32 [512, 8, 14], P('proc', 'rep'), may hold values from -1 to 511, as said below
- ladder_ints: bfloat16 [512, 8, 14, 128, 128], P('proc', 'rep'), may hold values from -0.046875 to 0.046875
- cycle_rows: int32 [512, 8, 8], P('proc', 'rep'), may hold values from 0 to 511, as said below
- cycle_ints: bfloat16 [512, 8, 8, 128, 128], P('proc', 'rep'), may hold values from -0.0625 to 0.0625
- bare_ints: bfloat16 [512, 208, 128], P('proc', 'rep'), may hold values from -6 to 6
- occ_energy: float32 [8, 208], replicated, may hold values from -2 to -0.5
- vir_energy: float32 [512, 128], P('proc'), may hold values from 0.5 to 4
- block_tiles: int32 [8], replicated, may hold values from 8 to 112, as said below
Outputs:
- new_amplitudes: bfloat16 [512, 208, 128], P('proc', 'rep')
Inputs may be any that keep to these rules, and one draw needn't show every extreme that they name: `block_tiles`: each entry is a multiple of 8; the entries sum to 512; the irreps' tiles lie one after another in irrep order; one irrep has 112 tiles. `ladder_rows`: for a column tile l of irrep g and an index r of the second dimension, the entries list, in some order, every tile k of irrep g with k % 8 == r once; the other entries are -1. The columns of the largest irrep fill all 14 entries. `cycle_rows`: every entry at index r of the second dimension is a tile k with k % 8 == r; entries may repeat.
All inputs are finite; a program needn't handle non-finite values.
Results may differ from a plain program's by a relative error of at most 0.001.
Values may be sent and summed in bfloat16 or wider, within the bound.
No kernel may reach another device: no remote copies, remote signals or barrier semaphores. Data moves between devices by JAX's collectives and lax.ppermute only.
A program may use at most 128 MiB of HBM per device.

v0:
```python
import jax
import jax.numpy as jnp
from jax import lax
from jax.sharding import PartitionSpec as P


def local(
    amplitudes,
    ladder_rows,
    ladder_ints,
    cycle_rows,
    cycle_ints,
    bare_ints,
    occ_energy,
    vir_energy,
    block_tiles,
):
    copies = lax.axis_size("rep")
    replica = lax.axis_index("rep")
    proc_index = lax.axis_index("proc")
    tiles_dev, pair_rows, tile_width = amplitudes.shape
    gathered = lax.all_gather(amplitudes, "proc", axis=0, tiled=True)
    ladder_list = ladder_rows[:, 0, :]
    usable = ladder_list >= 0
    ladder_tiles = gathered[jnp.maximum(ladder_list, 0)]
    ladder_tiles = jnp.where(
        usable[:, :, None, None], ladder_tiles, jnp.zeros((), ladder_tiles.dtype)
    )
    partial_value = jnp.einsum(
        "lsrk,lskc->lrc", ladder_tiles, ladder_ints[:, 0], preferred_element_type=jnp.float32
    )
    cycle_tiles = gathered[cycle_rows[:, 0, :]]
    partial_value = partial_value + jnp.einsum(
        "lsrk,lskc->lrc", cycle_tiles, cycle_ints[:, 0], preferred_element_type=jnp.float32
    )
    row_share = pair_rows // copies
    summed = lax.psum_scatter(partial_value, "rep", scatter_dimension=1, tiled=True)
    residual = bare_ints.astype(jnp.float32) + summed
    columns = proc_index * tiles_dev + jnp.arange(tiles_dev, dtype=jnp.int32)
    bounds = jnp.cumsum(block_tiles)
    irreps = jnp.sum((columns[:, None] >= bounds[None, :]).astype(jnp.int32), axis=1)
    selector = (
        irreps[:, None] == jnp.arange(block_tiles.shape[0], dtype=jnp.int32)[None, :]
    ).astype(jnp.float32)
    occ_rows = jnp.dot(selector, occ_energy, precision=lax.Precision.HIGHEST)
    occ_mine = lax.dynamic_slice_in_dim(occ_rows, replica * row_share, row_share, 1)
    denominator = vir_energy[:, None, :] - occ_mine[:, :, None]
    return (residual / denominator).astype(jnp.bfloat16)


def solution(mesh):
    return jax.shard_map(
        local,
        mesh=mesh,
        in_specs=(
            P("proc", None, None),
            P("proc", "rep", None),
            P("proc", "rep", None, None, None),
            P("proc", "rep", None),
            P("proc", "rep", None, None, None),
            P("proc", "rep", None),
            P(),
            P("proc", None),
            P(),
        ),
        out_specs=P("proc", "rep", None),
        check_vma=False,
    )
```

profile of v0, /device:TPU:2, one launch (start us, length us, event | category | flops | bytes accessed | tf_op | source)
XLA Modules:
  0.0 300.1 jit_solution(15536035518188840709)
XLA Ops:
  6.5 0.0 copy-start
  6.5 0.0 all-gather.2.cloned.1.call-start
  6.5 0.7 all-gather.2.cloned.1.call-update
  7.3 0.0 reduce-scatter.2.cloned.1.call-start
  7.3 0.7 compare_select_fusion
  8.0 0.1 copy.26
  8.1 0.1 reshape.90
  8.2 0.7 broadcast_maximum_fusion
  8.9 0.1 copy.25
  9.0 0.1 reshape.82
  9.0 0.7 broadcast_compare_fusion
  9.8 0.1 copy.31
  9.9 197.5 %all-gather.2.cloned.1.call-done = bf16[512,208,128]{2,1,0:T(8,128)(2,1)} async-done(((bf16[16,208,128]{2,1,0:T(8,128)(2,1)}), bf16[512,208,128]{2,1,0:T(8,128)(2,1)}) %all-gather.2.cloned.1.call-update) | async-done | bytes 27262992 | tf_op jit(solution)/shard_map/all_gather | solution.py:22
  207.4 12.9 %gather_fusion.1 = bf16[128,208,128]{2,1,0:T(8,128)(2,1)} fusion(bf16[512,208,128]{2,1,0:T(8,128)(2,1)} %all-gather.2.cloned.1.call-done, s32[1024]{0:T(1024)S(1)} %pad_clamp_fusion), kind=kCustom, calls=%fused_computation.1 | custom fusion | bytes 13632000 | tf_op jit(solution)/shard_map/gather | solution.py:32
  220.3 6.1 %fusion.5 = f32[16,208,128,1]{2,1,3,0:T(8,128)S(1)} fusion(bf16[16,8,208,128]{3,2,1,0:T(8,128)(2,1)} %bitcast.27, bf16[16,1,8,128,128]{4,3,2,1,0:T(8,128)(2,1)} %param.13), kind=kOutput, calls=%fused_computation.7 | convolution fusion | flops 872415232 | bytes 12713984 | tf_op jit(solution)/shard_map/lsrk,lskc->lrc/dot_general | solution.py:33
  226.4 19.3 %gather_fusion = bf16[224,208,128]{2,1,0:T(8,128)(2,1)} fusion(bf16[512,208,128]{2,1,0:T(8,128)(2,1)} %all-gather.2.cloned.1.call-done, s32[1024]{0:T(1024)S(1)} %pad_clamp_fusion.1), kind=kCustom, calls=%fused_computation | custom fusion | bytes 23856000 | tf_op jit(solution)/shard_map/gather | solution.py:25
  245.7 0.0 copy-start.3
  245.7 0.0 copy-start.1
  245.7 0.0 copy-start.2
  245.7 9.9 %bitcast_add_fusion = f32[16,208,128]{2,1,0:T(8,128)S(1)} fusion(f32[16,208,128,1]{2,1,3,0:T(8,128)S(1)} %fusion.5, bf16[16,1,14,128,128]{4,3,2,1,0:T(8,128)(2,1)} %param.11, bf16[16,14,208,128]{3,2,1,0:T(8,128)(2,1)} %bitcast.28, pred[16,14]{1,0:T(8,128)(4,1)S(1)} %bitcast.29), kind=kOutput, calls=%fused_computation.9 | convolution fusion | flops 1533116416 | bytes 22675680 | tf_op jit(solution)/shard_map/lsrk,lskc->lrc/dot_general | solution.py:29
  255.6 1.7 copy.27
  257.3 0.0 reduce-scatter.2.cloned.1.call-update
  257.3 0.0 copy-done.3
  257.3 0.2 reduce-window.8
  257.5 0.1 convert_reduce_fusion
  257.6 0.0 copy-done
  257.6 0.2 fusion.11
  257.8 0.1 constant_dynamic-slice_fusion
  257.9 0.1 copy.28
  258.0 33.6 %reduce-scatter.2.cloned.1.call-done = f32[16,26,128]{2,0,1:T(8,128)} async-done(((f32[16,208,128]{2,0,1:T(8,128)}), f32[16,26,128]{2,0,1:T(8,128)}) %reduce-scatter.2.cloned.1.call-update) | async-done | bytes 213008 | tf_op jit(solution)/shard_map/reduce_scatter | solution.py:37
  291.6 0.0 copy-done.1
  291.6 0.0 copy-done.2
  291.6 1.7 divide_convert_fusion
  (3 shorter events, 0.0 us)
Async XLA Ops:
  6.5 251.1 %copy-start = (f32[8,208]{1,0:T(8,128)S(1)}, f32[8,208]{1,0:T(8,128)}, u32[]{:S(2)}) copy-start(f32[8,208]{1,0:T(8,128)} %param.15) | copy-start | bytes 19972
  6.5 200.9 %all-gather.2.cloned.1.call-start = ((), (), s32[]{:S(2)}) async-start(), calls=%async_computation.1 | async-start | bytes 28114944 | tf_op jit(solution)/shard_map/all_gather | solution.py:22
  7.3 284.3 %reduce-scatter.2.cloned.1.call-start = ((), (), s32[]{:S(2)}) async-start(), calls=%async_computation.2 | async-start | bytes 1916928 | tf_op jit(solution)/shard_map/reduce_scatter | solution.py:37
  245.7 11.6 %copy-start.3 = (s32[8]{0:T(128)S(1)}, s32[8]{0:T(128)}, u32[]{:S(2)}) copy-start(s32[8]{0:T(128)} %param.17) | copy-start | bytes 100
  245.7 45.9 %copy-start.1 = (bf16[16,26,128]{2,0,1:T(8,128)(2,1)S(1)}, bf16[16,26,128]{2,0,1:T(8,128)(2,1)}, u32[]{:S(2)}) copy-start(bf16[16,26,128]{2,0,1:T(8,128)(2,1)} %param.14) | copy-start | bytes 319492
  245.7 45.9 %copy-start.2 = (f32[16,128]{1,0:T(8,128)S(1)}, f32[16,128]{1,0:T(8,128)}, u32[]{:S(2)}) copy-start(f32[16,128]{1,0:T(8,128)} %param.16) | copy-start | bytes 24580
Sparse Core Ops, SparseCore 0:
  9.9 197.4 all-gather.1
  257.4 34.0 reduce-scatter.1
where the time goes:
time: 300 us
  waiting for transfers between devices  232 us (77%)
  local copies, waits for them, and re-layouts  34.5 us (12%)
  matrix products  16.1 us (5%)
  between operations  13.4 us (4%)
  other arithmetic  4.1 us (1%)
    all_gather x1, waiting for transfers between devices, local(): gathered = lax.all_gather(amplitudes, 'proc', axis=0, tiled=True)  198 us
    reduce_scatter x1, waiting for transfers between devices, local(): lax.psum_scatter(partial_value, 'rep', scatter_dimension=1, tiled=True)  33.6 us
    gather x1, local copies, waits for them, and re-layouts, local(): ladder_tiles = gathered[jnp.maximum(ladder_list, 0)]  19.3 us
    gather x1, local copies, waits for them, and re-layouts, local(): cycle_tiles = gathered[cycle_rows[:, 0, :]]  12.9 us
    dot_general x1, matrix products, local(): jnp.einsum('lsrk,lskc->lrc', ladder_tiles, ladder_ints[:, 0], preferred_e...  9.86 us
    dot_general x1, matrix products, local(): jnp.einsum('lsrk,lskc->lrc', cycle_tiles, cycle_ints[:, 0], preferred_ele...  6.06 us
  transfers between devices with their start and end apart: 2, of which 2 were waited for; matrix products, arithmetic and copies ran while one was open for 1% of the time, Pallas kernels for 0%

commit v1 on v0

--- a/solution.py
+++ b/solution.py
@@ -19,7 +19,10 @@
     replica = lax.axis_index("rep")
     proc_index = lax.axis_index("proc")
     tiles_dev, pair_rows, tile_width = amplitudes.shape
-    gathered = lax.all_gather(amplitudes, "proc", axis=0, tiled=True)
+    gathered = jnp.concatenate(
+        jax.lax.all_to_all(jnp.stack([amplitudes] * jax.lax.axis_size("proc"), 0), "proc", 0, 0),
+        axis=0,
+    )
     ladder_list = ladder_rows[:, 0, :]
     usable = ladder_list >= 0
     ladder_tiles = gathered[jnp.maximum(ladder_list, 0)]

time: 300 us -> 786 us (2.62)
  waiting for transfers between devices: 232 us -> 697 us
  starting transfers between devices: 0.04 us -> 11.9 us
  local copies, waits for them, and re-layouts: 34.5 us -> 45 us
    all_to_all x0 -> x1, waiting for transfers between devices: none -> 628 us  [local(): jax.lax.all_to_all(jnp.stack([amplitudes] * jax.lax.axis_size('proc'), 0)...]
    all_gather x1 -> x0, waiting for transfers between devices: 198 us -> none  [local(): gathered = lax.all_gather(amplitudes, 'proc', axis=0, tiled=True)]
    reduce_scatter x1, waiting for transfers between devices: 33.6 us -> 69.4 us  [local(): lax.psum_scatter(partial_value, 'rep', scatter_dimension=1, tiled=True)]
    all_to_all x0 -> x1, starting transfers between devices: none -> 11.8 us  [local(): jax.lax.all_to_all(jnp.stack([amplitudes] * jax.lax.axis_size('proc'), 0)...]
    another operation x0 -> x1, local copies, waits for them, and re-layouts: none -> 10.5 us  [local(): jnp.stack([amplitudes] * jax.lax.axis_size('proc'), 0)]
  transfers between devices with their start and end apart: 2 -> 2, of which waited for: 2 -> 2; matrix products, arithmetic and copies ran while one was open for 1% -> 0% of each run, Pallas kernels for 0% -> 0%
where the time goes in v1:
time: 786 us
  waiting for transfers between devices  697 us (89%)
  local copies, waits for them, and re-layouts  45 us (6%)
  matrix products  16.1 us (2%)
  between operations  13.5 us (2%)
  starting transfers between devices  11.9 us (2%)
    all_to_all x1, waiting for transfers between devices, local(): jax.lax.all_to_all(jnp.stack([amplitudes] * jax.lax.axis_size('proc'), 0)...  628 us
    reduce_scatter x1, waiting for transfers between devices, local(): lax.psum_scatter(partial_value, 'rep', scatter_dimension=1, tiled=True)  69.4 us
    gather x1, local copies, waits for them, and re-layouts, local(): ladder_tiles = gathered[jnp.maximum(ladder_list, 0)]  19.3 us
  transfers between devices with their start and end apart: 2, of which 2 were waited for; matrix products, arithmetic and copies ran while one was open for 0% of the time, Pallas kernels for 0%

profile of v1, /device:TPU:2, one launch (start us, length us, event | category | flops | bytes accessed | tf_op | source)
XLA Modules:
  0.0 786.0 jit_solution(5117805349003620924)
XLA Ops:
  6.5 0.0 copy-start
  6.5 10.5 %stack.2 = bf16[32,16,208,128]{3,2,1,0:T(8,128)(2,1)} broadcast(bf16[16,208,128]{2,1,0:T(8,128)(2,1)} %param.9), dimensions={1,2,3} | broadcast | bytes 28114944 | tf_op jit(solution)/shard_map/stack | solution.py:23
  17.0 0.0 copy-start.4
  17.0 0.0 copy-start.2
  17.0 11.8 %all-to-all-start = ((bf16[32,16,208,128]{3,2,1,0:T(8,128)(2,1)}), bf16[32,16,208,128]{3,2,1,0:T(8,128)(2,1)}, u32[]{:S(2)}, u32[]{:S(2)}) async-start(bf16[32,16,208,128]{3,2,1,0:T(8,128)(2,1)} %stack.2), calls=%async_computation | async-start | bytes 54525952 | tf_op jit(solution)/shard_map/all_to_all | solution.py:23
  28.9 0.0 reduce-scatter.2.cloned.1.call-start
  28.9 0.0 copy-done.4
  28.9 0.1 copy.26
  29.0 0.1 reshape.96
  29.1 0.0 copy-done.2
  29.1 0.1 copy.25
  29.2 0.1 reshape.88
  29.3 0.1 copy.31
  29.4 628.1 %all-to-all-done = bf16[32,16,208,128]{3,2,1,0:T(8,128)(2,1)} async-done(((bf16[32,16,208,128]{3,2,1,0:T(8,128)(2,1)}), bf16[32,16,208,128]{3,2,1,0:T(8,128)(2,1)}, u32[]{:S(2)}, u32[]{:S(2)}) %all-to-all-start) | async-done | bytes 27263008 | tf_op jit(solution)/shard_map/all_to_all | solution.py:23
  657.5 12.9 %gather_fusion.1 = bf16[128,208,128]{2,1,0:T(8,128)(2,1)} fusion(bf16[512,208,128]{2,1,0:T(8,128)(2,1)} %bitcast.1, s32[1024]{0:T(1024)S(1)} %pad_clamp_fusion), kind=kCustom, calls=%fused_computation.1 | custom fusion | bytes 13632000 | tf_op jit(solution)/shard_map/gather | solution.py:35
  670.4 19.3 %gather_fusion = bf16[224,208,128]{2,1,0:T(8,128)(2,1)} fusion(bf16[512,208,128]{2,1,0:T(8,128)(2,1)} %bitcast.1, s32[1024]{0:T(1024)S(1)} %pad_clamp_fusion.1), kind=kCustom, calls=%fused_computation | custom fusion | bytes 23856000 | tf_op jit(solution)/shard_map/gather | solution.py:28
  689.7 6.0 fusion.5
  695.8 0.0 copy-start.5
  695.8 0.0 copy-start.1
  695.8 0.0 copy-start.3
  695.8 9.8 %bitcast_add_fusion = f32[16,208,128]{2,1,0:T(8,128)S(1)} fusion(f32[16,208,128,1]{2,1,3,0:T(8,128)S(1)} %fusion.5, bf16[16,1,14,128,128]{4,3,2,1,0:T(8,128)(2,1)} %param.11, bf16[16,14,208,128]{3,2,1,0:T(8,128)(2,1)} %bitcast.29, pred[16,14]{1,0:T(8,128)(4,1)S(1)} %bitcast.30), kind=kOutput, calls=%fused_computation.9 | convolution fusion | flops 1533116416 | bytes 22675680 | tf_op jit(solution)/shard_map/lsrk,lskc->lrc/dot_general | solution.py:32
  705.6 1.7 copy.27
  707.4 0.0 reduce-scatter.2.cloned.1.call-update
  707.4 0.0 copy-done.5
  707.4 0.2 reduce-window.8
  707.6 0.1 convert_reduce_fusion
  707.7 0.0 copy-done
  707.7 0.2 fusion.11
  707.9 0.1 constant_dynamic-slice_fusion
  707.9 0.1 copy.28
  708.0 69.4 %reduce-scatter.2.cloned.1.call-done = f32[16,26,128]{2,0,1:T(8,128)} async-done(((f32[16,208,128]{2,0,1:T(8,128)}), f32[16,26,128]{2,0,1:T(8,128)}) %reduce-scatter.2.cloned.1.call-update) | async-done | bytes 213008 | tf_op jit(solution)/shard_map/reduce_scatter | solution.py:40
  777.4 0.0 copy-done.1
  777.4 0.0 copy-done.3
  777.4 1.7 divide_convert_fusion
  (6 shorter events, 0.0 us)
Async XLA Ops:
  6.5 701.1 %copy-start = (f32[8,208]{1,0:T(8,128)S(1)}, f32[8,208]{1,0:T(8,128)}, u32[]{:S(2)}) copy-start(f32[8,208]{1,0:T(8,128)} %param.15) | copy-start | bytes 19972
  17.0 11.9 %copy-start.4 = (s32[16,1,8]{0,2,1:T(8,128)S(1)}, s32[16,1,8]{0,2,1:T(8,128)}, u32[]{:S(2)}) copy-start(s32[16,1,8]{0,2,1:T(8,128)} %param.12) | copy-start | bytes 1540
  17.0 12.1 %copy-start.2 = (s32[16,1,14]{0,1,2:T(1,128)S(1)}, s32[16,1,14]{0,1,2:T(1,128)}, u32[]{:S(2)}) copy-start(s32[16,1,14]{0,1,2:T(1,128)} %param.10) | copy-start | bytes 2692
  17.0 640.4 %all-to-all-start = ((bf16[32,16,208,128]{3,2,1,0:T(8,128)(2,1)}), bf16[32,16,208,128]{3,2,1,0:T(8,128)(2,1)}, u32[]{:S(2)}, u32[]{:S(2)}) async-start(bf16[32,16,208,128]{3,2,1,0:T(8,128)(2,1)} %stack.2), calls=%async_computation | async-start | bytes 54525952 | tf_op jit(solution)/shard_map/all_to_all | solution.py:23
  28.9 748.5 %reduce-scatter.2.cloned.1.call-start = ((), (), s32[]{:S(2)}) async-start(), calls=%async_computation.2 | async-start | bytes 1916928 | tf_op jit(solution)/shard_map/reduce_scatter | solution.py:40
  695.8 11.6 %copy-start.5 = (s32[8]{0:T(128)S(1)}, s32[8]{0:T(128)}, u32[]{:S(2)}) copy-start(s32[8]{0:T(128)} %param.17) | copy-start | bytes 100
  695.8 81.6 %copy-start.1 = (bf16[16,26,128]{2,0,1:T(8,128)(2,1)S(1)}, bf16[16,26,128]{2,0,1:T(8,128)(2,1)}, u32[]{:S(2)}) copy-start(bf16[16,26,128]{2,0,1:T(8,128)(2,1)} %param.14) | copy-start | bytes 319492
  695.8 81.6 %copy-start.3 = (f32[16,128]{1,0:T(8,128)S(1)}, f32[16,128]{1,0:T(8,128)}, u32[]{:S(2)}) copy-start(f32[16,128]{1,0:T(8,128)} %param.16) | copy-start | bytes 24580
Sparse Core Ops, SparseCore 0:
  707.5 69.8 reduce-scatter.1
